TPU v7x, 32 devices: a whole 2x2x4 slice. The times are simulated.
32 devices in a mesh: row: 8 (over y, x, core), col: 4 (over z).
Axes of the slice: x: 2, y: 2, z: 4, core: 2. Of those that a mesh axis runs over, the one named last changes fastest.
Arguments:
- front_matrix: bfloat16 [20480, 20480], P('row', 'col'), may hold values from -37 to 37
- right_samples: bfloat16 [20480, 256], P('col'), may hold values from -0.0390625 to 0.0390625
- left_samples: bfloat16 [20480, 256], P('row'), may hold values from -0.0390625 to 0.0390625
Outputs:
- residual: bfloat16 [20480, 20480], P('row', 'col')
- core_scaled: float32 [256, 256], replicated
All inputs are finite; a program needn't handle non-finite values.
Results may differ from a plain program's by a relative error of at most 0.0035.
Values may be sent and summed in bfloat16 or wider, within the bound.
A program may use at most 128 MiB of HBM per device.

v0:
```python
import functools
import math

import jax
import jax.numpy as jnp
from jax import lax
from jax.experimental import pallas as pl
from jax.experimental.pallas import tpu as pltpu
from jax.sharding import PartitionSpec as P

F32 = jnp.float32
BF16 = jnp.bfloat16
BASE = 64


def mm(a, b, dims=((1,), (0,))):
    return lax.dot_general(
        a, b, (dims, ((), ())), precision=lax.Precision.HIGHEST, preferred_element_type=F32
    )


def base_inverse(grams):
    size = grams[0].shape[0]
    tall = size // 8
    width = 2 * size
    eye = (
        lax.broadcasted_iota(jnp.int32, (size, size), 0) == lax.broadcasted_iota(jnp.int32, (size, size), 1)
    ).astype(F32)
    wide = [jnp.concatenate([g, eye], axis=1) for g in grams]
    parts = [[w[8 * t : 8 * t + 8] for t in range(tall)] for w in wide]
    sub = lax.broadcasted_iota(jnp.int32, (8, width), 0)
    for k in range(size):
        top, at = k // 8, k % 8
        for part in parts:
            row = part[top][at : at + 1, :]
            scaled = row * (1.0 / row[:, k : k + 1])
            for t in range(top, tall):
                col = part[t][:, k : k + 1]
                if t == top:
                    if at == 7:
                        continue
                    part[t] = part[t] - jnp.where(sub > at, col * scaled, 0.0)
                else:
                    part[t] = part[t] - col * scaled
    out = []
    for part in parts:
        full = jnp.concatenate(part, axis=0)
        left, right = full[:, :size], full[:, size:]
        pivot = jnp.sum(left * eye, axis=1, keepdims=True)
        out.append(right * lax.rsqrt(pivot))
    return out


def inverse_factors(grams):
    size = grams[0].shape[0]
    if size <= BASE:
        return base_inverse(grams)
    half = size // 2
    first = inverse_factors([g[:half, :half] for g in grams])
    lower = [mm(g[half:, :half], w, ((1,), (1,))) for g, w in zip(grams, first)]
    rest = [g[half:, half:] - mm(l, l, ((1,), (1,))) for g, l in zip(grams, lower)]
    second = inverse_factors(rest)
    out = []
    for w1, l21, w2 in zip(first, lower, second):
        below = -mm(w2, mm(l21, w1))
        out.append(
            jnp.concatenate(
                [
                    jnp.concatenate([w1, jnp.zeros_like(w1)], axis=1),
                    jnp.concatenate([below, w2], axis=1),
                ],
                axis=0,
            )
        )
    return out


def factor_kernel(order, total_ref, core_ref, middle_ref):
    size = core_ref.shape[0]
    gram_r, cross, gram_c = (total_ref[:, n].reshape(size, size) for n in range(3))
    w_r, w_c = inverse_factors([gram_r, gram_c])
    core = mm(mm(w_r, cross), w_c, ((1,), (1,)))
    core_ref[...] = core / jnp.sqrt(F32(order))
    middle_ref[...] = mm(mm(w_r, core, ((0,), (0,))), w_c)


def factor(total, order):
    size = total.shape[-1]
    shape = jax.ShapeDtypeStruct((size, size), F32)
    return pl.pallas_call(
        functools.partial(factor_kernel, order),
        out_shape=(shape, shape),
        in_specs=[pl.BlockSpec(memory_space=pltpu.VMEM)],
        out_specs=(pl.BlockSpec(memory_space=pltpu.VMEM),) * 2,
    )(total)


def split(x):
    high = x.astype(BF16)
    return high, (x - high.astype(F32)).astype(BF16)


def dot(a, b, dims=((1,), (0,))):
    return lax.dot_general(a, b, (dims, ((), ())), preferred_element_type=F32)


def greet(groups):
    barrier = pltpu.get_barrier_semaphore()
    for axis, count in groups:
        me = lax.axis_index(axis)
        for step in range(1, count):
            pl.semaphore_signal(
                barrier, inc=1, device_id={axis: lax.rem(me + step, count)}, device_id_type=pl.DeviceIdType.MESH
            )
    pl.semaphore_wait(barrier, sum(count - 1 for _, count in groups))


def scatter(axis, count, source, slots, send, recv):
    me = lax.axis_index(axis)
    copies = []
    for step in range(1, count):
        peer = lax.rem(me + step, count)
        copies.append(
            pltpu.make_async_remote_copy(
                src_ref=source(peer),
                dst_ref=slots.at[step - 1],
                send_sem=send.at[step - 1],
                recv_sem=recv.at[step - 1],
                device_id={axis: peer},
                device_id_type=pl.DeviceIdType.MESH,
            )
        )
    for copy in copies:
        copy.start()
    return copies


def gather(axis, count, blocks, send, recv):
    me = lax.axis_index(axis)
    sends, receives = [], []
    for step in range(1, count):
        for slot, peer, bag in (
            (me, lax.rem(me + step, count), sends),
            (lax.rem(me - step + count, count), lax.rem(me + step, count), receives),
        ):
            bag.append(
                pltpu.make_async_remote_copy(
                    src_ref=blocks.at[me],
                    dst_ref=blocks.at[slot],
                    send_sem=send.at[step - 1],
                    recv_sem=recv.at[step - 1],
                    device_id={axis: peer},
                    device_id_type=pl.DeviceIdType.MESH,
                )
            )
    for copy in sends:
        copy.start()
    return sends, receives


def finish(pair):
    for copy in pair[1]:
        copy.wait_recv()
    for copy in pair[0]:
        copy.wait_send()


def hop(source, target, send, recv, peer):
    return pltpu.make_async_remote_copy(
        src_ref=source,
        dst_ref=target,
        send_sem=send,
        recv_sem=recv,
        device_id={"col": peer},
        device_id_type=pl.DeviceIdType.MESH,
    )


def chain_step(step, cols, yp_ref, bufs, send, recv):
    me = lax.axis_index("col")
    for way in range(2):
        place = me if way == 0 else cols - 1 - me
        to = me + 1 if way == 0 else me - 1
        far = cols - 1 - (step - place)
        chunk = far if way == 0 else cols - 1 - far
        buf, s_sem, r_sem = bufs[way], send.at[way, step], recv.at[way, step]

        @pl.when(place == 0)
        def _():
            hop(yp_ref.at[chunk], buf.at[step], s_sem, r_sem, to).start()

        if step > 0:

            @pl.when((place >= 1) & (place <= step))
            def _():
                hop(buf.at[step - 1], buf.at[step - 1], send.at[way, step - 1], recv.at[way, step - 1], to).wait_recv()
                buf[step - 1] = buf[step - 1] + yp_ref[chunk]
                hop(buf.at[step - 1], buf.at[step], s_sem, r_sem, to).start()


def chain_end(cols, yp_ref, y_ref, acc, bufs, send, recv):
    me = lax.axis_index("col")
    last = cols - 2
    acc[...] = yp_ref[me]
    for way in range(2):
        place = me if way == 0 else cols - 1 - me
        came = me - 1 if way == 0 else me + 1
        buf = bufs[way]

        @pl.when(place >= 1)
        def _():
            hop(buf.at[last], buf.at[last], send.at[way, last], recv.at[way, last], came).wait_recv()
            acc[...] = acc[...] + buf[last]

    y_ref[me] = acc[...].astype(BF16)
    for way in range(2):
        place = me if way == 0 else cols - 1 - me
        to = me + 1 if way == 0 else me - 1
        for step in range(cols - 1):

            @pl.when(place <= step)
            def _():
                hop(acc, bufs[way].at[step], send.at[way, step], recv.at[way, step], to).wait_send()


def spread(cols, y_ref, send, recv):
    me = lax.axis_index("col")

    def each(step, act):
        for way in range(2):
            place = me if way == 0 else cols - 1 - me
            sign = 1 if way == 0 else -1
            s_sem, r_sem = send.at[way, step], recv.at[way, step]
            if act == "got":

                @pl.when(place >= step + 1)
                def _():
                    block = y_ref.at[me - sign * (step + 1)]
                    hop(block, block, s_sem, r_sem, me - sign).wait_recv()

            else:

                @pl.when((place >= step) & (place < cols - 1))
                def _():
                    block = y_ref.at[me - sign * step]
                    copy = hop(block, block, s_sem, r_sem, me + sign)
                    if act == "send":
                        copy.start()
                    else:
                        copy.wait_send()

    for step in range(cols - 1):
        each(step, "send")
        each(step, "got")
    for step in range(cols - 1):
        each(step, "sent")


def share_kernel(
    rows, cols, tile, yp_ref, left_ref, front_ref, y_ref, z_ref, zp, z_buf, right_buf, left_buf, acc, tiles, t_sem, *sems
):
    greet((("row", rows), ("col", cols)))
    me_r = lax.axis_index("row")
    chain = (cols, yp_ref, (right_buf, left_buf), sems[2], sems[3])
    z_rows, size = zp.shape[1:]
    count = front_ref.shape[1] // tile
    group = tile // z_rows

    def fetch(t):
        slot = lax.rem(t, 2)
        return pltpu.make_async_copy(
            front_ref.at[:, pl.ds(pl.multiple_of(t * tile, 128), tile)], tiles.at[slot], t_sem.at[slot]
        )

    chain_step(0, *chain)
    fetch(0).start()

    @pl.loop(0, count)
    def _(t):
        @pl.when(t + 1 < count)
        def _():
            fetch(t + 1).start()

        fetch(t).wait()
        part = dot(left_ref[...], tiles[lax.rem(t, 2)]).T.astype(BF16)
        for n in range(group):
            zp[t * group + n] = part[n * z_rows : (n + 1) * z_rows]

    z_in = scatter("row", rows, lambda k: zp.at[k], z_buf, sems[0], sems[1])
    for step in range(1, cols - 1):
        chain_step(step, *chain)
    for copy in z_in:
        copy.wait()
    total = zp[me_r].astype(F32)
    for step in range(rows - 1):
        total = total + z_buf[step].astype(F32)
    z_ref[me_r] = total.astype(BF16)
    z_out = gather("row", rows, z_ref, sems[4], sems[5])
    chain_end(cols, yp_ref, y_ref, acc, (right_buf, left_buf), sems[2], sems[3])
    spread(cols, y_ref, sems[6], sems[7])
    finish(z_out)


def share(yp, left, front, rows):
    cols, y_rows, size = yp.shape
    depth, width = front.shape
    z_rows = width // rows
    tile = z_rows * 128 // math.gcd(z_rows, 128)
    dma = pltpu.SemaphoreType.DMA
    vmem = pl.BlockSpec(memory_space=pltpu.VMEM)
    return pl.pallas_call(
        functools.partial(share_kernel, rows, cols, tile),
        out_shape=(jax.ShapeDtypeStruct(yp.shape, BF16), jax.ShapeDtypeStruct((rows, z_rows, size), BF16)),
        in_specs=[vmem, vmem, pl.BlockSpec(memory_space=pl.ANY)],
        out_specs=(vmem, vmem),
        scratch_shapes=[
            pltpu.VMEM((rows, z_rows, size), BF16),
            pltpu.VMEM((rows - 1, z_rows, size), BF16),
            pltpu.VMEM((cols - 1, y_rows, size), F32),
            pltpu.VMEM((cols - 1, y_rows, size), F32),
            pltpu.VMEM((y_rows, size), F32),
            pltpu.VMEM((2, depth, tile), BF16),
            dma((2,)),
            dma((rows - 1,)),
            dma((rows - 1,)),
            dma((2, cols - 1)),
            dma((2, cols - 1)),
            dma((rows - 1,)),
            dma((rows - 1,)),
            dma((2, cols - 1)),
            dma((2, cols - 1)),
        ],
        compiler_params=pltpu.CompilerParams(collective_id=0, has_side_effects=True),
    )(yp, left, front)


def total_kernel(rows, cols, both_ref, gram_ref, total_ref, row_buf, own, col_buf, *sems):
    greet((("row", rows), ("col", cols)))
    me_r, me_c = lax.axis_index("row"), lax.axis_index("col")
    height = gram_ref.shape[0]

    def piece(k):
        return both_ref.at[:, pl.ds(pl.multiple_of(k * height, 8), height), :]

    for copy in scatter("row", rows, piece, row_buf, sems[0], sems[1]):
        copy.wait()
    summed = piece(me_r)[...]
    for step in range(rows - 1):
        summed = summed + row_buf[step]
    total_ref[me_r, 0] = summed[0]
    own[0] = summed[1]
    own[1] = gram_ref[...]
    col_buf[cols - 1] = own[...]
    for copy in scatter("col", cols, lambda k: own, col_buf, sems[2], sems[3]):
        copy.wait()
    summed = None
    for member in range(cols):
        slot = lax.rem(me_c - member + 2 * cols - 1, cols)
        summed = col_buf[slot] if summed is None else summed + col_buf[slot]
    total_ref[me_r, 1] = summed[0]
    total_ref[me_r, 2] = summed[1]
    finish(gather("row", rows, total_ref, sems[4], sems[5]))


def total_of(both, gram, rows, cols):
    height, size = gram.shape
    dma = pltpu.SemaphoreType.DMA
    return pl.pallas_call(
        functools.partial(total_kernel, rows, cols),
        out_shape=jax.ShapeDtypeStruct((rows, 3, height, size), F32),
        in_specs=[pl.BlockSpec(memory_space=pltpu.VMEM)] * 2,
        out_specs=pl.BlockSpec(memory_space=pltpu.VMEM),
        scratch_shapes=[
            pltpu.VMEM((rows - 1, 2, height, size), F32),
            pltpu.VMEM((2, height, size), F32),
            pltpu.VMEM((cols, 2, height, size), F32),
        ]
        + [dma((n - 1,)) for n in (rows, rows, cols, cols, rows, rows)],
        compiler_params=pltpu.CompilerParams(collective_id=1, has_side_effects=True),
    )(both, gram)


def body(order, rows, cols, front, right, left):
    size = right.shape[1]
    yp = dot(front, right).reshape(cols, -1, size)
    y, z = share(yp, left.T, front, rows)
    y, z = y.reshape(-1, size), z.reshape(-1, size)
    high, low = split(dot(front, z))
    both = jnp.stack([dot(y, y, ((0,), (0,))), dot(y, high, ((0,), (0,))) + dot(y, low, ((0,), (0,)))])
    height = size // rows
    gram = lax.dynamic_slice_in_dim(dot(z, z, ((0,), (0,))), lax.axis_index("row") * height, height)
    core_scaled, middle = factor(total_of(both, gram, rows, cols), order)
    high, low = split(middle)
    projected = (dot(y, high) + dot(y, low)).astype(BF16)
    update = dot(projected, z, ((1,), (1,)))
    residual = (front.astype(F32) - update).astype(BF16)
    return residual, core_scaled


def solution(mesh):
    in_specs = (P("row", "col"), P("col", None), P("row", None))
    out_specs = (P("row", "col"), P())

    def run(front, right, left):
        inner = functools.partial(body, front.shape[0], mesh.shape["row"], mesh.shape["col"])
        return jax.shard_map(inner, mesh=mesh, in_specs=in_specs, out_specs=out_specs, check_vma=False)(
            front, right, left
        )

    return run
```

profile of v0, /device:TPU:0, one launch (start us, length us, event | category | flops | bytes accessed | tf_op | source)
XLA Modules:
  0.0 201.6 jit_solution(2540467295857590456)
XLA Ops:
  0.6 0.0 copy-start
  0.7 2.6 %copy.5 = bf16[2560,256]{0,1:T(8,128)(2,1)} copy(bf16[2560,256]{1,0:T(8,128)(2,1)} %param.5) | data formatting | bytes 2621440 | tf_op args[2]
  3.2 0.0 copy-done
  3.2 13.5 %fusion.9 = f32[2560,256]{1,0:T(8,128)} fusion(bf16[2560,5120]{1,0:T(8,128)(2,1)} %front_ref.1, bf16[5120,256]{1,0:T(8,128)(2,1)S(1)} %copy-done), kind=kOutput, calls=%fused_computation.18 | convolution fusion | flops 6710886400 | bytes 31457280 | tf_op jit(solution)/shard_map/dot_general | solution.py:104
  16.8 80.5 %shard_map.50 = (bf16[4,640,256]{2,1,0:T(8,128)(2,1)}, bf16[8,640,256]{2,1,0:T(8,128)(2,1)}) custom-call(f32[4,640,256]{2,1,0:T(8,128)} %bitcast.33, bf16[256,2560]{1,0:T(8,128)(2,1)} %bitcast.30, bf16[2560,5120]{1,0:T(8,128)(2,1)} %front_ref.1), custom_call_target="tpu_custom_call" | custom-call | tf_op jit(solution)/shard_map/pallas_call | solution.py:311
  97.3 0.0 copy-start.5
  97.3 2.4 %convolution_bitcast_fusion.2 = f32[1,256,256]{2,1,0:T(8,128)S(1)} fusion(bf16[4,640,256]{2,1,0:T(8,128)(2,1)} %get-tuple-element.6), kind=kOutput, calls=%fused_computation.9 | convolution fusion | flops 335544320 | bytes 1572864 | tf_op jit(solution)/shard_map/dot_general | solution.py:104
  99.7 0.1 copy-done.5
  99.8 0.9 convolution_bitcast_fusion.1
  100.7 0.6 constant_dynamic-slice_fusion.gram_ref
  101.3 0.0 copy-start.2
  101.3 14.0 %convolution_bitcast_fusion = f32[2560,256]{0,1:T(8,128)} fusion(bf16[5120,256]{1,0:T(8,128)(2,1)} %bitcast.31, bf16[2560,5120]{1,0:T(8,128)(2,1)} %front_ref.1), kind=kOutput, calls=%fused_computation.2 | convolution fusion | flops 6710886400 | bytes 31457280 | tf_op jit(solution)/shard_map/dot_general | solution.py:104
  115.3 0.0 copy-done.2
  115.3 0.0 copy-start.3
  115.3 3.3 %fusion.1 = f32[256,256]{1,0:T(8,128)S(1)} fusion(bf16[2560,256]{1,0:T(8,128)(2,1)S(1)} %bitcast.27, f32[2560,256]{0,1:T(8,128)} %convolution_bitcast_fusion), kind=kOutput, calls=%fused_computation.5 | convolution fusion | flops 338165760 | bytes 4194304 | tf_op jit(solution)/shard_map/dot_general | solution.py:104
  118.5 0.0 copy-done.3
  118.6 0.6 fusion.2
  119.2 0.8 pad_maximum_fusion.both_ref
  120.0 29.6 %shard_map.51.total_ref = f32[8,3,32,256]{3,2,1,0:T(8,128)} custom-call(f32[2,256,256]{2,1,0:T(8,128)} %pad_maximum_fusion.both_ref, f32[32,256]{1,0:T(8,128)} %constant_dynamic-slice_fusion.gram_ref), custom_call_target="tpu_custom_call" | custom-call | tf_op jit(solution)/shard_map/pallas_call | solution.py:368
  149.6 28.1 %shard_map.52 = (f32[256,256]{1,0:T(8,128)}, f32[256,256]{1,0:T(8,128)}) custom-call(f32[8,3,32,256]{3,2,1,0:T(8,128)} %shard_map.51.total_ref), custom_call_target="tpu_custom_call" | custom-call | tf_op jit(solution)/shard_map/pallas_call | solution.py:90
  177.7 0.0 copy-start.4
  177.7 3.0 %fusion.7 = f32[2560,256]{1,0:T(8,128)} fusion(bf16[2560,256]{1,0:T(8,128)(2,1)S(1)} %bitcast.29, f32[256,256]{1,0:T(8,128)} %get-tuple-element.8), kind=kOutput, calls=%fused_computation.15 | convolution fusion | flops 335609856 | bytes 4194304 | tf_op jit(solution)/shard_map/dot_general | solution.py:104
  180.7 0.0 copy-done.4
  180.7 0.0 copy-start.1
  180.7 20.9 %subtract_convert_fusion = bf16[2560,5120]{1,0:T(8,128)(2,1)} fusion(bf16[2560,5120]{1,0:T(8,128)(2,1)} %front_ref.1, bf16[5120,256]{1,0:T(8,128)(2,1)} %bitcast.32, f32[2560,256]{1,0:T(8,128)} %fusion.7, bf16[2560,256]{1,0:T(8,128)(2,1)} %bitcast.26, f32[256,256]{1,0:T(8,128)S(1)} %copy-done.4), kind=kOutput, calls=%fused_computation | convolution fusion | flops 7087325184 | bytes 59244544 | tf_op jit(solution)/shard_map/dot_general | solution.py:104
  201.6 0.0 copy-done.1
Async XLA Ops:
  0.6 2.6 %copy-start = (bf16[5120,256]{1,0:T(8,128)(2,1)S(1)}, bf16[5120,256]{1,0:T(8,128)(2,1)}, u32[]{:S(2)}) copy-start(bf16[5120,256]{1,0:T(8,128)(2,1)} %param.4) | copy-start | bytes 7864324
  97.3 2.5 %copy-start.5 = (bf16[8,640,256]{2,1,0:T(8,128)(2,1)S(1)}, bf16[8,640,256]{2,1,0:T(8,128)(2,1)}, u32[]{:S(2)}) copy-start(bf16[8,640,256]{2,1,0:T(8,128)(2,1)} %get-tuple-element.7) | copy-start | bytes 7864324
  101.3 14.0 %copy-start.2 = (bf16[4,640,256]{2,1,0:T(8,128)(2,1)S(1)}, bf16[4,640,256]{2,1,0:T(8,128)(2,1)}, u32[]{:S(2)}) copy-start(bf16[4,640,256]{2,1,0:T(8,128)(2,1)} %get-tuple-element.6) | copy-start | bytes 3932164
  115.3 3.3 %copy-start.3 = (f32[2560,256]{0,1:T(8,128)S(1)}, f32[2560,256]{0,1:T(8,128)}, u32[]{:S(2)}) copy-start(f32[2560,256]{0,1:T(8,128)} %convolution_bitcast_fusion) | copy-start | bytes 7864324
  177.7 3.0 %copy-start.4 = (f32[256,256]{1,0:T(8,128)S(1)}, f32[256,256]{1,0:T(8,128)}, u32[]{:S(2)}) copy-start(f32[256,256]{1,0:T(8,128)} %get-tuple-element.8) | copy-start | bytes 786436
  180.7 20.9 %copy-start.1 = (bf16[5120,256]{1,0:T(8,128)(2,1)S(1)}, bf16[5120,256]{1,0:T(8,128)(2,1)}, u32[]{:S(2)}) copy-start(bf16[5120,256]{1,0:T(8,128)(2,1)} %param.4) | copy-start | bytes 7864324
where the time goes:
time: 203 us; the launch traced here: 202 us
  Pallas kernels  138 us (68%)
  matrix products  58.5 us (29%)
  local copies, waits for them, and re-layouts  3.37 us (2%)
    pallas_call x1, Pallas kernels, share(): pl.pallas_call(functools.partial(share_kernel, rows, cols, tile), out_sha...  80.5 us
    dot_general x8, matrix products, dot(): return lax.dot_general(a, b, (dims, ((), ())), preferred_element_type=F32)  58.5 us
    pallas_call x1, Pallas kernels, total_of(): pl.pallas_call(functools.partial(total_kernel, rows, cols), out_shape=jax...  29.6 us
    pallas_call x1, Pallas kernels, factor(): pl.pallas_call(functools.partial(factor_kernel, order), out_shape=(shape,...  28.1 us

commit v1 on v0

v1 whole, which is shorter than its diff:
```python
import functools
import math

import jax
import jax.numpy as jnp
from jax import lax
from jax.experimental import pallas as pl
from jax.experimental.pallas import tpu as pltpu
from jax.sharding import PartitionSpec as P

F32 = jnp.float32
BF16 = jnp.bfloat16
BASE = 64
CHUNKS = 10
LAG = 2
RING = 4
MIB = 1024 * 1024


def mm(a, b, dims=((1,), (0,))):
    return lax.dot_general(
        a, b, (dims, ((), ())), precision=lax.Precision.HIGHEST, preferred_element_type=F32
    )


def base_inverse(grams):
    size = grams[0].shape[0]
    tall = size // 8
    width = 2 * size
    eye = (
        lax.broadcasted_iota(jnp.int32, (size, size), 0) == lax.broadcasted_iota(jnp.int32, (size, size), 1)
    ).astype(F32)
    wide = [jnp.concatenate([g, eye], axis=1) for g in grams]
    parts = [[w[8 * t : 8 * t + 8] for t in range(tall)] for w in wide]
    sub = lax.broadcasted_iota(jnp.int32, (8, width), 0)
    for k in range(size):
        top, at = k // 8, k % 8
        for part in parts:
            row = part[top][at : at + 1, :]
            scaled = row * (1.0 / row[:, k : k + 1])
            for t in range(top, tall):
                col = part[t][:, k : k + 1]
                if t == top:
                    if at == 7:
                        continue
                    part[t] = part[t] - jnp.where(sub > at, col * scaled, 0.0)
                else:
                    part[t] = part[t] - col * scaled
    out = []
    for part in parts:
        full = jnp.concatenate(part, axis=0)
        left, right = full[:, :size], full[:, size:]
        pivot = jnp.sum(left * eye, axis=1, keepdims=True)
        out.append(right * lax.rsqrt(pivot))
    return out


def inverse_factors(grams):
    size = grams[0].shape[0]
    if size <= BASE:
        return base_inverse(grams)
    half = size // 2
    first = inverse_factors([g[:half, :half] for g in grams])
    lower = [mm(g[half:, :half], w, ((1,), (1,))) for g, w in zip(grams, first)]
    rest = [g[half:, half:] - mm(l, l, ((1,), (1,))) for g, l in zip(grams, lower)]
    second = inverse_factors(rest)
    out = []
    for w1, l21, w2 in zip(first, lower, second):
        below = -mm(w2, mm(l21, w1))
        out.append(
            jnp.concatenate(
                [
                    jnp.concatenate([w1, jnp.zeros_like(w1)], axis=1),
                    jnp.concatenate([below, w2], axis=1),
                ],
                axis=0,
            )
        )
    return out


def split(x):
    high = x.astype(BF16)
    return high, (x - high.astype(F32)).astype(BF16)


def dot(a, b, dims=((1,), (0,))):
    return lax.dot_general(a, b, (dims, ((), ())), preferred_element_type=F32)


def remote(source, target, send, recv, where):
    return pltpu.make_async_remote_copy(
        src_ref=source,
        dst_ref=target,
        send_sem=send,
        recv_sem=recv,
        device_id=where,
        device_id_type=pl.DeviceIdType.MESH,
    )


def spread(axis, count, source, slots, send, recv):
    me = lax.axis_index(axis)
    copies = []
    for step in range(1, count):
        peer = lax.rem(me + step, count)
        copies.append(remote(source(peer), slots.at[step - 1], send.at[step - 1], recv.at[step - 1], {axis: peer}))
    for copy in copies:
        copy.start()
    return copies


def gather(count, block, send, recv):
    me = lax.axis_index("row")
    sends, receives = [], []
    for step in range(1, count):
        for slot, bag in ((me, sends), (lax.rem(me - step + count, count), receives)):
            peer = {"row": lax.rem(me + step, count)}
            bag.append(remote(block(me), block(slot), send.at[step - 1], recv.at[step - 1], peer))
    for copy in sends:
        copy.start()
    return sends, receives


def sketch_kernel(rows, cols, steps, *refs):
    front, right, left = refs[:3]
    yhi, zt, total = refs[3:6]
    f_ref, r_buf, lt, yown, y_in, y_out, zp, z_core, z_sum, z_in, t_acc, cross, gram, slab, row_buf, own, col_buf = refs[6:23]
    (f_sem, io_sem, core_s, core_r, fin_s, fin_r, ph_s, ph_r, ch_s, ch_r, rs_s, rs_r, cs_s, cs_r, ag_s, ag_r) = refs[23:]
    n = steps
    depth, width = f_ref.shape
    size = yhi.shape[1]
    half = size // 2
    quart = size // 4
    dh, cw = depth // n, width // n
    phases = z_sum.shape[0]
    last = cols - 1
    span = size // rows
    me_r, me_c = lax.axis_index("row"), lax.axis_index("col")
    core = lax.rem(me_r, 2)

    barrier = pltpu.get_barrier_semaphore()
    for axis, count in (("row", rows), ("col", cols)):
        me = lax.axis_index(axis)
        for step in range(1, count):
            pl.semaphore_signal(
                barrier, inc=1, device_id={axis: lax.rem(me + step, count)}, device_id_type=pl.DeviceIdType.MESH
            )

    def shell(k):
        down = (pl.ds(k * dh, depth - k * dh), pl.ds(k * cw, cw))
        out = [pltpu.make_async_copy(front.at[down], f_ref.at[down], f_sem.at[0, k])]
        if k + 1 < n:
            over = (pl.ds(k * dh, dh), pl.ds((k + 1) * cw, width - (k + 1) * cw))
            out.append(pltpu.make_async_copy(front.at[over], f_ref.at[over], f_sem.at[1, k]))
        return out

    load_l = pltpu.make_async_copy(left, yhi, io_sem.at[0])
    load_r = pltpu.make_async_copy(right, r_buf, io_sem.at[1])
    load_l.start()
    first = shell(0)
    first[0].start()
    load_r.start()
    for copy in first[1:] + shell(1):
        copy.start()
    t_acc[...] = jnp.zeros_like(t_acc)
    gram[...] = jnp.zeros_like(gram)
    slab[...] = jnp.zeros_like(slab)
    load_l.wait()

    @pl.loop(0, depth // 128)
    def _(i):
        at = pl.ds(pl.multiple_of(i * 128, 128), 128)
        lt[:, at] = yhi[at, :].astype(F32).T.astype(BF16)

    def flip(bit):
        return {"row": me_r + bit - 2 * bit * lax.rem(lax.div(me_r, bit), 2)}

    bits = [2 << q for q in range(phases)]
    paths = (bits, bits[::-1])

    def cols_of(k):
        return pl.ds(pl.multiple_of(k * cw, cw), cw)

    def rows_of(k):
        return pl.ds(pl.multiple_of(k * dh, dh), dh)

    def core_copy(k):
        slot = lax.rem(k, RING)
        return remote(zp.at[slot, 1 - core], z_core.at[k], core_s.at[k], core_r.at[k], flip(1))

    def phase_copy(q, way, k):
        return remote(
            z_sum.at[q, way, lax.rem(k, RING)], z_in.at[q, way, k], ph_s.at[q, way, k], ph_r.at[q, way, k], flip(paths[way][q])
        )

    def final_copy(k):
        return remote(zt.at[k, core], zt.at[k, core], fin_s.at[k], fin_r.at[k], flip(1))

    def final_wait(k):
        other = zt.at[k, 1 - core]
        remote(other, other, fin_s.at[k], fin_r.at[k], flip(1)).wait_recv()

    def chain_copy(way, k):
        to = lax.rem(me_c + (1 if way == 0 else last), cols)
        return remote(
            y_out.at[way, lax.rem(k, RING)], y_in.at[way, k], ch_s.at[way, k], ch_r.at[way, k], {"col": to}
        )

    def compute(k):
        for s in range(n):

            @pl.when(k == s)
            def _():
                for copy in shell(s):
                    copy.wait()
                if s + 2 < n:
                    for copy in shell(s + 2):
                        copy.start()

        @pl.when(k >= RING)
        def _():
            core_copy(k - RING).wait_send()

        slot = lax.rem(k, RING)
        part = dot(lt[...], f_ref[:, cols_of(k)]).astype(BF16)
        zp[slot, 0] = part[:half]
        zp[slot, 1] = part[half:]

        @pl.when(k == 0)
        def _():
            load_r.wait()

        yown[k] = dot(f_ref[rows_of(k), :], r_buf[...])

    def push_chain(way, k, place, value):
        @pl.when(k >= RING)
        def _():
            chain_copy(way, k - RING).wait_send()

        y_out[way, lax.rem(k, RING)] = value.astype(BF16)
        chain_copy(way, k).start()

    def send_phase(q, k, value):
        @pl.when(k >= RING)
        def _():
            for way in range(2):
                phase_copy(q, way, k - RING).wait_send()

        z_sum[q, 0, lax.rem(k, RING)] = value[:quart]
        z_sum[q, 1, lax.rem(k, RING)] = value[quart:]
        for way in range(2):
            phase_copy(q, way, k).start()

    def arrived(q, k):
        parts = []
        for way in range(2):
            phase_copy(q, way, k).wait_recv()
            parts.append((z_sum[q, way, lax.rem(k, RING)].astype(F32) + z_in[q, way, k].astype(F32)).astype(BF16))
        return jnp.concatenate(parts, axis=0)

    def inside(k, body):
        @pl.when((k >= 0) & (k < n))
        def _():
            body(k)

    compute(0)
    pl.semaphore_wait(barrier, rows + cols - 2)

    z_lag = LAG * phases
    y_lag = LAG * last
    row_tile = math.gcd(depth, 640)

    @pl.loop(0, n + max(z_lag + 1, y_lag))
    def _(t):
        @pl.when(t < n)
        def _():
            core_copy(t).start()
            for way in range(2):
                place = me_c if way == 0 else last - me_c

                @pl.when(place == 0)
                def _():
                    push_chain(way, t, place, yown[t])

        @pl.when(t + 1 < n)
        def _():
            compute(t + 1)

        @pl.when(t < n)
        def _():
            core_copy(t).wait_recv()
            mine = zp[lax.rem(t, RING), core].astype(F32) + z_core[t].astype(F32)
            send_phase(0, t, mine.astype(BF16))

        for q in range(1, phases):
            inside(t - LAG * q, lambda k: send_phase(q, k, arrived(q - 1, k)))

        for way in range(2):
            place = me_c if way == 0 else last - me_c
            k = t - LAG * place

            @pl.when((place > 0) & (k >= 0) & (k < n))
            def _():
                chain_copy(way, k).wait_recv()

                @pl.when(place < last)
                def _():
                    push_chain(way, k, place, yown[k] + y_in[way, k].astype(F32))

        def z_final(k):
            zt[k, core] = arrived(phases - 1, k)
            final_copy(k).start()

        inside(t - z_lag, z_final)

        def y_final(k):
            for way in range(2):
                place = me_c if way == 0 else last - me_c

                @pl.when(place > 0)
                def _():
                    yown[k] = yown[k] + y_in[way, k].astype(F32)

            value = yown[k]
            high, low = split(value)
            yhi[rows_of(k), :] = high

            @pl.when(lax.rem(k, cols) == me_c)
            def _():
                across_high, across_low = split(value.T)
                gram[...] = gram[...] + (dot(across_high, high) + (dot(across_high, low) + dot(across_low, high)))

        inside(t - y_lag, y_final)

        def z_use(k):
            final_wait(k)
            block = zt[k].reshape(size, cw)
            at = me_r * span
            piece = zt[k, lax.div(at, half), pl.ds(pl.multiple_of(lax.rem(at, half), span), span), :]
            slab[...] = slab[...] + dot(piece, block, ((1,), (1,)))

            @pl.loop(0, depth // row_tile)
            def _(i):
                at = pl.ds(pl.multiple_of(i * row_tile, row_tile), row_tile)
                t_acc[at, :] = t_acc[at, :] + dot(f_ref[at, cols_of(k)], block, ((1,), (1,)))

        inside(t - z_lag - 1, z_use)

    def piece_of(ref):
        return lambda k: ref.at[pl.ds(pl.multiple_of(k * span, span), span), :]

    def row_sum(m, ref, copies):
        for copy in copies:
            copy.wait()
        value = piece_of(ref)(me_r)[...]
        for step in range(rows - 1):
            value = value + row_buf[m, step]
        return value

    def col_send(m, value):
        own[m] = value
        col_buf[m, cols - 1] = value
        return spread("col", cols, lambda k: own.at[m], col_buf.at[m], cs_s.at[m], cs_r.at[m])

    def col_sum(m, copies):
        for copy in copies:
            copy.wait()
        value = None
        for member in range(cols):
            slot = lax.rem(me_c - member + 2 * cols - 1, cols)
            value = col_buf[m, slot] if value is None else value + col_buf[m, slot]
        total[me_r, m] = value
        return gather(rows, lambda k: total.at[k, m], ag_s.at[m], ag_r.at[m])

    gram_rows = spread("row", rows, piece_of(gram), row_buf.at[0], rs_s.at[0], rs_r.at[0])
    slab_cols = col_send(2, slab[...])
    cross[...] = jnp.zeros_like(cross)

    @pl.loop(0, n)
    def _(k):
        high, low = split(t_acc[rows_of(k), :])
        across_high, across_low = split(yown[k].T)
        cross[...] = cross[...] + (dot(across_high, high) + (dot(across_high, low) + dot(across_low, high)))

    cross_rows = spread("row", rows, piece_of(cross), row_buf.at[1], rs_s.at[1], rs_r.at[1])
    gram_cols = col_send(0, row_sum(0, gram, gram_rows))
    slab_all = col_sum(2, slab_cols)
    cross_cols = col_send(1, row_sum(1, cross, cross_rows))
    gram_all = col_sum(0, gram_cols)
    cross_all = col_sum(1, cross_cols)

    @pl.loop(0, n)
    def _(k):
        final_copy(k).wait_send()

    @pl.loop(max(n - RING, 0), n)
    def _(k):
        core_copy(k).wait_send()
        for q in range(phases):
            for way in range(2):
                phase_copy(q, way, k).wait_send()
        for way in range(2):
            place = me_c if way == 0 else last - me_c

            @pl.when(place < last)
            def _():
                chain_copy(way, k).wait_send()

    for sends, receives in (slab_all, gram_all, cross_all):
        for copy in receives:
            copy.wait_recv()
        for copy in sends:
            copy.wait_send()


def sketch(front, right, left, rows, cols):
    depth, width = front.shape
    size = right.shape[1]
    n = CHUNKS
    while width % (128 * n) or depth % (16 * n):
        n -= 1
    phases = rows.bit_length() - 2
    half, quart, span = size // 2, size // 4, size // rows
    dh, cw = depth // n, width // n
    dma = pltpu.SemaphoreType.DMA
    vmem = pl.BlockSpec(memory_space=pltpu.VMEM)
    hbm = pl.BlockSpec(memory_space=pl.ANY)
    return pl.pallas_call(
        functools.partial(sketch_kernel, rows, cols, n),
        out_shape=(
            pltpu.VMEM((depth, size), BF16),
            pltpu.VMEM((n, 2, half, cw), BF16),
            pltpu.VMEM((rows, 3, span, size), F32),
        ),
        in_specs=[hbm] * 3,
        out_specs=(vmem,) * 3,
        scratch_shapes=[
            pltpu.VMEM((depth, width), BF16),
            pltpu.VMEM((width, size), BF16),
            pltpu.VMEM((size, depth), BF16),
            pltpu.VMEM((n, dh, size), F32),
            pltpu.VMEM((2, n, dh, size), BF16),
            pltpu.VMEM((2, RING, dh, size), BF16),
            pltpu.VMEM((RING, 2, half, cw), BF16),
            pltpu.VMEM((n, half, cw), BF16),
            pltpu.VMEM((phases, 2, RING, quart, cw), BF16),
            pltpu.VMEM((phases, 2, n, quart, cw), BF16),
            pltpu.VMEM((depth, size), F32),
            pltpu.VMEM((size, size), F32),
            pltpu.VMEM((size, size), F32),
            pltpu.VMEM((span, size), F32),
            pltpu.VMEM((2, rows - 1, span, size), F32),
            pltpu.VMEM((3, span, size), F32),
            pltpu.VMEM((3, cols, span, size), F32),
            dma((2, n)),
            dma((2,)),
            dma((n,)),
            dma((n,)),
            dma((n,)),
            dma((n,)),
            dma((phases, 2, n)),
            dma((phases, 2, n)),
            dma((2, n)),
            dma((2, n)),
            dma((2, rows - 1)),
            dma((2, rows - 1)),
            dma((3, cols - 1)),
            dma((3, cols - 1)),
            dma((3, rows - 1)),
            dma((3, rows - 1)),
        ],
        compiler_params=pltpu.CompilerParams(collective_id=0, has_side_effects=True, vmem_limit_bytes=58 * MIB),
    )(front, right, left)


def finish_kernel(order, tile, front, total_ref, y_ref, z_ref, out_ref, core_ref, f_ref, p_ref, in_sem, out_sem):
    load = pltpu.make_async_copy(front, f_ref, in_sem)
    load.start()
    size = core_ref.shape[0]
    depth = f_ref.shape[0]
    n, _, _, cw = z_ref.shape
    gram_r, cross, gram_c = (total_ref[:, m].reshape(size, size) for m in range(3))
    w_r, w_c = inverse_factors([gram_r, gram_c])
    core = mm(mm(w_r, cross), w_c, ((1,), (1,)))
    core_ref[...] = core / jnp.sqrt(F32(order))
    high, low = split(mm(mm(w_r, core, ((0,), (0,))), w_c))
    p_ref[...] = (dot(y_ref[...], high) + dot(y_ref[...], low)).astype(BF16)
    load.wait()
    per = depth // tile

    def spot(i):
        at = pl.ds(pl.multiple_of(lax.rem(i, per) * tile, 16), tile)
        return at, pl.ds(pl.multiple_of(lax.div(i, per) * cw, 128), cw)

    def store(i):
        at, cols = spot(i)
        return pltpu.make_async_copy(f_ref.at[at, cols], out_ref.at[at, cols], out_sem.at[i])

    @pl.loop(0, n * per)
    def _(i):
        at, cols = spot(i)
        update = dot(p_ref[at, :], z_ref[lax.div(i, per)].reshape(size, cw))
        f_ref[at, cols] = (f_ref[at, cols].astype(F32) - update).astype(BF16)
        store(i).start()

    @pl.loop(0, n * per)
    def _(i):
        store(i).wait()


def finish(front, total, y, z, order):
    depth, width = front.shape
    size = y.shape[1]
    n = z.shape[0]
    tile = math.gcd(depth, 1280)
    vmem = pl.BlockSpec(memory_space=pltpu.VMEM)
    hbm = pl.BlockSpec(memory_space=pl.ANY)
    return pl.pallas_call(
        functools.partial(finish_kernel, order, tile),
        out_shape=(jax.ShapeDtypeStruct((depth, width), BF16), jax.ShapeDtypeStruct((size, size), F32)),
        in_specs=[hbm, vmem, vmem, vmem],
        out_specs=(hbm, vmem),
        scratch_shapes=[
            pltpu.VMEM((depth, width), BF16),
            pltpu.VMEM((depth, size), BF16),
            pltpu.SemaphoreType.DMA,
            pltpu.SemaphoreType.DMA((n * (depth // tile),)),
        ],
        compiler_params=pltpu.CompilerParams(vmem_limit_bytes=36 * MIB),
    )(front, total, y, z)


def body(order, rows, cols, front, right, left):
    y, z, total = sketch(front, right, left, rows, cols)
    return finish(front, total, y, z, order)


def solution(mesh):
    in_specs = (P("row", "col"), P("col", None), P("row", None))
    out_specs = (P("row", "col"), P())

    def run(front, right, left):
        inner = functools.partial(body, front.shape[0], mesh.shape["row"], mesh.shape["col"])
        return jax.shard_map(inner, mesh=mesh, in_specs=in_specs, out_specs=out_specs, check_vma=False)(
            front, right, left
        )

    return run
```

time: 203 us -> 133 us (0.66)
  matrix products: 58.5 us -> 0 us
  Pallas kernels: 138 us -> 132 us
  local copies, waits for them, and re-layouts: 3.37 us -> 0 us
    dot_general x8 -> x0, matrix products: 58.5 us -> none  [dot(): return lax.dot_general(a, b, (dims, ((), ())), preferred_element_type=F32)]
    pallas_call x3 -> x2, Pallas kernels: 138 us -> 132 us  [the longest x1 84.7 us: sketch(): pl.pallas_call(functools.partial(sketch_kernel, rows, cols, n), out_shape...]
    unnamed x13 -> x0, local copies, waits for them, and re-layouts: 2.75 us -> none
where the time goes in v1:
time: 133 us
  Pallas kernels  132 us (99%)
    pallas_call x1, Pallas kernels, sketch(): pl.pallas_call(functools.partial(sketch_kernel, rows, cols, n), out_shape...  84.7 us
    pallas_call x1, Pallas kernels, finish(): pl.pallas_call(functools.partial(finish_kernel, order, tile), out_shape=(...  47.4 us

profile of v1, /device:TPU:0, one launch (start us, length us, event | category | flops | bytes accessed | tf_op | source)
XLA Modules:
  0.0 132.9 jit_solution(37113499861878204)
XLA Ops:
  0.6 84.7 %shard_map.50 = (bf16[2560,256]{1,0:T(8,128)(2,1)S(1)}, bf16[10,2,128,512]{3,2,1,0:T(8,128)(2,1)S(1)}, f32[8,3,32,256]{3,2,1,0:T(8,128)S(1)}) custom-call(bf16[2560,5120]{1,0:T(8,128)(2,1)} %front.1, bf16[5120,256]{1,0:T(8,128)(2,1)} %refs_1_.1, bf16[2560,256]{1,0:T(8,128)(2,1)} %refs_2_.1), custom_call_target="tpu_custom_call" | custom-call | tf_op jit(solution)/shard_map/pallas_call | solution.py:429
  85.4 47.4 %shard_map.51 = (bf16[2560,5120]{1,0:T(8,128)(2,1)}, f32[256,256]{1,0:T(8,128)}) custom-call(bf16[2560,5120]{1,0:T(8,128)(2,1)} %front.1, f32[8,3,32,256]{3,2,1,0:T(8,128)S(1)} %get-tuple-element.5.total_ref, bf16[2560,256]{1,0:T(8,128)(2,1)S(1)} %get-tuple-element.6.y_ref, bf16[10,2,128,512]{3,2,1,0:T(8,128)(2,1)S(1)} %get-tuple-element.7.z_ref), custom_call_target="tpu_custom_call" | custom-call | tf_op jit(solution)/shard_map/pallas_call | solution.py:519

commit v2 on v1

--- a/solution.py
+++ b/solution.py
@@ -27,32 +27,34 @@
     size = grams[0].shape[0]
     tall = size // 8
     width = 2 * size
-    eye = (
-        lax.broadcasted_iota(jnp.int32, (size, size), 0) == lax.broadcasted_iota(jnp.int32, (size, size), 1)
-    ).astype(F32)
+    eye = (lax.broadcasted_iota(jnp.int32, (size, size), 0) == lax.broadcasted_iota(jnp.int32, (size, size), 1)).astype(F32)
     wide = [jnp.concatenate([g, eye], axis=1) for g in grams]
     parts = [[w[8 * t : 8 * t + 8] for t in range(tall)] for w in wide]
     sub = lax.broadcasted_iota(jnp.int32, (8, width), 0)
-    for k in range(size):
-        top, at = k // 8, k % 8
-        for part in parts:
-            row = part[top][at : at + 1, :]
-            scaled = row * (1.0 / row[:, k : k + 1])
-            for t in range(top, tall):
-                col = part[t][:, k : k + 1]
-                if t == top:
-                    if at == 7:
-                        continue
-                    part[t] = part[t] - jnp.where(sub > at, col * scaled, 0.0)
-                else:
-                    part[t] = part[t] - col * scaled
-    out = []
-    for part in parts:
-        full = jnp.concatenate(part, axis=0)
-        left, right = full[:, :size], full[:, size:]
-        pivot = jnp.sum(left * eye, axis=1, keepdims=True)
-        out.append(right * lax.rsqrt(pivot))
-    return out
+    out = [[] for _ in grams]
+    for p in range(tall):
+        for part, done in zip(parts, out):
+            block = part[p]
+            cols = [jnp.broadcast_to(block[:, 8 * p + j : 8 * p + j + 1], (8, width)) for j in range(8)]
+            side = [[jnp.broadcast_to(part[t][:, 8 * p + j : 8 * p + j + 1], (8, width)) for j in range(8)] for t in range(p + 1, tall)]
+            keep = block
+            for k in range(8):
+                inverse = 1.0 / cols[k][k : k + 1, :]
+                pivot_row = block[k : k + 1, :]
+                keep = jnp.where(sub == k, pivot_row * lax.rsqrt(cols[k][k : k + 1, :]), keep)
+                scaled = pivot_row * inverse
+                column = cols[k]
+                block = jnp.where(sub == k, scaled, block - column * scaled)
+                for j in range(k + 1, 8):
+                    ratio = cols[j][k : k + 1, :] * inverse
+                    cols[j] = jnp.where(sub == k, ratio, cols[j] - column * ratio)
+            done.append(keep)
+            for s, t in zip(side, range(p + 1, tall)):
+                acc = part[t]
+                for k in range(8):
+                    acc = acc - s[k] * block[k : k + 1, :]
+                part[t] = acc
+    return [jnp.concatenate(done, axis=0)[:, size:] for done in out]
 
 
 def inverse_factors(grams):
@@ -513,7 +515,7 @@
     depth, width = front.shape
     size = y.shape[1]
     n = z.shape[0]
-    tile = math.gcd(depth, 1280)
+    tile = math.gcd(depth, 2560)
     vmem = pl.BlockSpec(memory_space=pltpu.VMEM)
     hbm = pl.BlockSpec(memory_space=pl.ANY)
     return pl.pallas_call(

time: 133 us -> 118 us (0.89)
  Pallas kernels: 132 us -> 117 us
    pallas_call x1, Pallas kernels: 47.4 us -> 32.7 us  [finish(): pl.pallas_call(functools.partial(finish_kernel, order, tile), out_shape=(...]
where the time goes in v2:
time: 118 us
  Pallas kernels  117 us (99%)
    pallas_call x1, Pallas kernels, sketch(): pl.pallas_call(functools.partial(sketch_kernel, rows, cols, n), out_shape...  84.7 us
    pallas_call x1, Pallas kernels, finish(): pl.pallas_call(functools.partial(finish_kernel, order, tile), out_shape=(...  32.7 us

profile of v2, /device:TPU:0, one launch (start us, length us, event | category | flops | bytes accessed | tf_op | source)
XLA Modules:
  0.0 118.3 jit_solution(14768694599168128578)
XLA Ops:
  0.6 84.7 %shard_map.50 = (bf16[2560,256]{1,0:T(8,128)(2,1)S(1)}, bf16[10,2,128,512]{3,2,1,0:T(8,128)(2,1)S(1)}, f32[8,3,32,256]{3,2,1,0:T(8,128)S(1)}) custom-call(bf16[2560,5120]{1,0:T(8,128)(2,1)} %front.1, bf16[5120,256]{1,0:T(8,128)(2,1)} %refs_1_.1, bf16[2560,256]{1,0:T(8,128)(2,1)} %refs_2_.1), custom_call_target="tpu_custom_call" | custom-call | tf_op jit(solution)/shard_map/pallas_call | solution.py:431
  85.4 32.7 %shard_map.51 = (bf16[2560,5120]{1,0:T(8,128)(2,1)}, f32[256,256]{1,0:T(8,128)}) custom-call(bf16[2560,5120]{1,0:T(8,128)(2,1)} %front.1, f32[8,3,32,256]{3,2,1,0:T(8,128)S(1)} %get-tuple-element.5.total_ref, bf16[2560,256]{1,0:T(8,128)(2,1)S(1)} %get-tuple-element.6.y_ref, bf16[10,2,128,512]{3,2,1,0:T(8,128)(2,1)S(1)} %get-tuple-element.7.z_ref), custom_call_target="tpu_custom_call" | custom-call | tf_op jit(solution)/shard_map/pallas_call | solution.py:521
